TPU v7x, 256 devices: a whole 4x4x8 slice. The times are simulated.
256 devices in a mesh: rcv: 32 (over z, x_hi, core), frq: 8 (over x_lo, y).
Axes of the slice: x: 4 (x_hi: 2, x_lo: 2; x = x_hi * 2 + x_lo), y: 4, z: 8, core: 2. Of those that a mesh axis runs over, the one named last changes fastest.
Arguments:
- spectra: bfloat16 [2, 256, 128, 8192], P(None, None, 'frq', 'rcv'), may hold values from -6 to 6
- virtual_sources: int32 [128], replicated, may hold values from 0 to 8191, as said below
- references: int32 [256], replicated, may hold values from 0 to 8191, as said below
- coda_start: int32 [128], replicated, may hold values from 64 to 255
- coda_end: int32 [128], replicated, may hold values from 384 to 511
Outputs:
- correlations: float32 [2, 128, 256, 8192], P(None, 'frq', None, 'rcv')
Inputs may be any that keep to these rules, and one draw needn't show every extreme that they name: `virtual_sources`: distinct receivers; virtual source v is one of the receivers (v // 4) * 256 to (v // 4 + 1) * 256 - 1. `references`: distinct receivers; reference p is one of the receivers (p // 8) * 256 to (p // 8 + 1) * 256 - 1.
All inputs are finite; a program needn't handle non-finite values.
Results may differ from a plain program's by a relative error of at most 0.0068.
Values may be sent and summed in bfloat16 or wider, within the bound.
A program may use at most 64 MiB of HBM per device.

v0:
```python
import math

import jax
import jax.numpy as jnp
from jax import lax
from jax.sharding import PartitionSpec as P

L = 1024


def lag_tables(freq_count, lag_count, first_lag, lag_width):
    lag_values = first_lag + jnp.arange(lag_width, dtype=jnp.int32)
    bin_numbers = jnp.arange(freq_count, dtype=jnp.int32) + 1
    phase_steps = bin_numbers[:, None] * lag_values[None, :] % lag_count
    angles = phase_steps.astype(jnp.float32) * (2.0 * math.pi / lag_count)
    return (jnp.cos(angles), jnp.sin(angles))


def taper_weights(coda_start, coda_end, lag_count):
    lag_values = jnp.arange(lag_count, dtype=jnp.int32)
    lag_reach = jnp.where(lag_values < lag_count // 2, lag_values, lag_count - lag_values)[:, None]
    coda_first = coda_start[None, :]
    coda_last = coda_end[None, :]
    inside = (lag_reach >= coda_first) & (lag_reach < coda_last)
    window_span = (coda_last - coda_first).astype(jnp.float32)
    sine_value = jnp.sin(
        math.pi * ((lag_reach - coda_first).astype(jnp.float32) + 0.5) / window_span
    )
    return jnp.where(inside, sine_value * sine_value, jnp.zeros_like(sine_value))


def recompress(spectra_block, taper_table, lag_count):
    freq_count = spectra_block.shape[1]
    src_count = spectra_block.shape[2]
    rcv_count = spectra_block.shape[3]
    flattened = spectra_block.reshape(2 * freq_count, src_count * rcv_count)
    lag_width = min(lag_count, 256)
    accumulated = jnp.zeros((2 * freq_count, src_count * rcv_count), jnp.float32)
    for lag_block in range(lag_count // lag_width):
        first_lag = lag_block * lag_width
        cosine_table, sine_table = lag_tables(freq_count, lag_count, first_lag, lag_width)
        stacked = jnp.concatenate([cosine_table, -sine_table], axis=0)
        inverse = (stacked.T * (1.0 / math.sqrt(freq_count))).astype(jnp.bfloat16)
        forward = (stacked * (4.0 / math.sqrt(lag_count))).astype(jnp.bfloat16)
        series = jnp.dot(inverse, flattened, preferred_element_type=jnp.float32)
        weights = taper_table[first_lag : first_lag + lag_width]
        shaped = series.reshape(lag_width, src_count, rcv_count) * weights[:, :, None]
        squashed = (shaped / jnp.sqrt(1.0 + shaped * shaped)).astype(jnp.bfloat16)
        squashed = squashed.reshape(lag_width, src_count * rcv_count)
        accumulated = accumulated + jnp.dot(forward, squashed, preferred_element_type=jnp.float32)
    return accumulated.astype(jnp.bfloat16).reshape(2, freq_count, src_count, rcv_count)


def cross_spectra(sources, spectra_block):
    window_count = spectra_block.shape[1]
    left_side = jnp.concatenate([sources[0], sources[1]], axis=0)
    right_real = jnp.concatenate([spectra_block[0], spectra_block[1]], axis=0)
    right_imag = jnp.concatenate([spectra_block[1], -spectra_block[0]], axis=0)
    real_part = jnp.einsum(
        "wfv,wfr->fvr", left_side, right_real, preferred_element_type=jnp.float32
    )
    imag_part = jnp.einsum(
        "wfv,wfr->fvr", left_side, right_imag, preferred_element_type=jnp.float32
    )
    return (jnp.stack([real_part, imag_part]) / math.sqrt(window_count)).astype(jnp.bfloat16)


def recorrelate(picked, relayed):
    src_total = picked.shape[2]
    left_side = jnp.concatenate([picked[0], picked[1]], axis=1)
    right_real = jnp.concatenate([relayed[0], relayed[1]], axis=1)
    right_imag = jnp.concatenate([relayed[1], -relayed[0]], axis=1)
    real_part = jnp.einsum(
        "fvp,fvr->fpr", left_side, right_real, preferred_element_type=jnp.float32
    )
    imag_part = jnp.einsum(
        "fvp,fvr->fpr", left_side, right_imag, preferred_element_type=jnp.float32
    )
    return jnp.stack([real_part, imag_part]) / math.sqrt(src_total)


def per_device(spectra, virtual_sources, references, coda_start, coda_end):
    rcv_dev = spectra.shape[3]
    rcv_index = lax.axis_index("rcv")
    first_rcv = rcv_index * rcv_dev
    local_rows = jnp.arange(rcv_dev, dtype=jnp.int32)
    onehot = (local_rows[:, None] == (virtual_sources - first_rcv)[None, :]).astype(jnp.bfloat16)
    selected = jnp.einsum("cwfr,rv->cwfv", spectra, onehot, preferred_element_type=jnp.float32)
    sources = lax.psum(selected.astype(jnp.bfloat16), "rcv")
    cross_spec = cross_spectra(sources, spectra)
    taper_table = taper_weights(coda_start, coda_end, L)
    spread = lax.all_to_all(cross_spec, "frq", split_axis=3, concat_axis=1, tiled=True)
    relaid = recompress(spread, taper_table, L)
    returned = lax.all_to_all(relaid, "frq", split_axis=1, concat_axis=3, tiled=True)
    ref_onehot = (local_rows[:, None] == (references - first_rcv)[None, :]).astype(jnp.bfloat16)
    ref_terms = jnp.einsum(
        "cfvr,rp->cfvp", returned, ref_onehot, preferred_element_type=jnp.float32
    )
    picked = lax.psum(ref_terms.astype(jnp.bfloat16), "rcv")
    return recorrelate(picked, returned)


def solution(mesh):
    return jax.shard_map(
        per_device,
        mesh=mesh,
        in_specs=(P(None, None, "frq", "rcv"), P(), P(), P(), P()),
        out_specs=P(None, "frq", None, "rcv"),
        check_vma=False,
    )
```

profile of v0, /device:TPU:1, one launch (start us, length us, event | category | flops | bytes accessed | tf_op | source)
XLA Modules:
  0.0 701.1 jit_solution(8071123630282561780)
XLA Ops:
  7.2 5.2 convert_bitcast_fusion
  12.4 3.7 copy.89
  16.3 2.3 slice_bitcast_fusion.1
  18.6 272.0 %all-reduce.3.cloned.1.call-done = bf16[2,256,16,128]{1,3,2,0:T(8,128)(2,1)} async-done(((bf16[2,256,16,128]{1,3,2,0:T(8,128)(2,1)}), bf16[2,256,16,128]{1,3,2,0:T(8,128)(2,1)}) %all-reduce.3.cloned.1.call-update) | async-done | bytes 2097168 | tf_op jit(solution)/shard_map/psum | solution.py:89
  290.6 1.9 slice_bitcast_fusion.5
  293.4 1.3 fusion.19
  294.7 1.3 fusion.16
  296.6 3.1 copy.92
  299.7 4.5 all-to-all-start
  304.3 1.9 multiply_select_fusion
  306.9 2.1 fusion.65
  309.0 21.4 %all-to-all-done = bf16[2,16,128,256]{2,1,0,3:T(8,128)(2,1)S(1)} async-done(((bf16[2,16,128,256]{2,1,0,3:T(8,128)(2,1)}), bf16[2,16,128,256]{2,1,0,3:T(8,128)(2,1)S(1)}, u32[]{:S(2)}, u32[]{:S(2)}) %all-to-all-start) | async-done | bytes 2097184 | tf_op jit(solution)/shard_map/all_to_all | solution.py:92
  330.4 5.8 copy.94
  336.2 10.7 %reshape.66 = bf16[256,4096]{1,0:T(8,128)(2,1)S(1)} reshape(bf16[2,8,16,128,32]{4,3,2,1,0:T(8,128)(2,1)} %copy.94) | data formatting | bytes 4194304 | tf_op jit(solution)/shard_map/reshape | solution.py:36
  346.9 2.6 copy.95
  349.5 4.2 multiply_convert_fusion.2
  353.7 1.2 copy.99
  355.3 2.6 multiply_convert_fusion.1
  359.1 2.6 multiply_convert_fusion.3
  362.9 2.8 multiply_convert_fusion
  369.2 2.1 fusion
  371.2 3.3 copy.104
  374.5 2.0 reshape.71
  376.5 5.2 copy.105
  381.7 3.8 all-to-all-start.1
  385.5 26.1 %all-to-all-done.1 = bf16[2,128,128,32]{2,3,0,1:T(8,128)(2,1)S(1)} async-done(((bf16[2,128,128,32]{2,3,0,1:T(8,128)(2,1)}), bf16[2,128,128,32]{2,3,0,1:T(8,128)(2,1)S(1)}, u32[]{:S(2)}, u32[]{:S(2)}) %all-to-all-start.1) | async-done | bytes 2097184 | tf_op jit(solution)/shard_map/all_to_all | solution.py:94
  412.3 2.1 convolution_convert_fusion
  414.7 1.3 fusion.90
  417.0 1.3 copy.109
  419.1 266.9 %all-reduce.5.cloned.1.call-done = bf16[2,16,128,256]{3,2,1,0:T(8,128)(2,1)} async-done(((bf16[2,16,128,256]{3,2,1,0:T(8,128)(2,1)}), bf16[2,16,128,256]{3,2,1,0:T(8,128)(2,1)}) %all-reduce.5.cloned.1.call-update) | async-done | bytes 2097168 | tf_op jit(solution)/shard_map/psum | solution.py:99
  685.9 1.7 slice_bitcast_fusion.3
  689.7 4.1 maximum_multiply_fusion
  (40 shorter events, 14.0 us)
Async XLA Ops:
  6.5 284.0 %all-reduce.3.cloned.1.call-start = ((), (), s32[]{:S(2)}) async-start(), calls=%async_computation.2 | async-start | bytes 4194304 | tf_op jit(solution)/shard_map/psum | solution.py:89
  290.6 2.2 copy-start.1
  290.6 2.9 copy-start.2
  299.7 4.5 copy-start.4
  299.7 4.6 copy-start.5
  299.7 30.7 %all-to-all-start = ((bf16[2,16,128,256]{2,1,0,3:T(8,128)(2,1)}), bf16[2,16,128,256]{2,1,0,3:T(8,128)(2,1)S(1)}, u32[]{:S(2)}, u32[]{:S(2)}) async-start(bf16[2,16,128,256]{2,1,0,3:T(8,128)(2,1)} %copy.92), calls=%async_computation | async-start | bytes 4194304 | tf_op jit(solution)/shard_map/all_to_all | solution.py:92
  353.7 1.6 copy-start
  381.7 3.8 copy-start.3
  381.7 29.9 %all-to-all-start.1 = ((bf16[2,128,128,32]{2,3,0,1:T(8,128)(2,1)}), bf16[2,128,128,32]{2,3,0,1:T(8,128)(2,1)S(1)}, u32[]{:S(2)}, u32[]{:S(2)}) async-start(bf16[2,128,128,32]{2,3,0,1:T(8,128)(2,1)} %copy.105), calls=%async_computation.1 | async-start | bytes 4194304 | tf_op jit(solution)/shard_map/all_to_all | solution.py:94
  385.5 300.5 %all-reduce.5.cloned.1.call-start = ((), (), s32[]{:S(2)}) async-start(), calls=%async_computation.3 | async-start | bytes 4194304 | tf_op jit(solution)/shard_map/psum | solution.py:99
Sparse Core Ops, SparseCore 0:
  12.5 277.9 all-reduce.2
  414.5 271.4 all-reduce.4
where the time goes:
time: 710 us; the launch traced here: 701 us
  waiting for transfers between devices  586 us (83%)
  local copies, waits for them, and re-layouts  54.1 us (8%)
  matrix products  28.4 us (4%)
  between operations  14.1 us (2%)
  other arithmetic  9.79 us (1%)
  starting transfers between devices  8.31 us (1%)
    psum x1, waiting for transfers between devices, per_device(): sources = lax.psum(selected.astype(jnp.bfloat16), 'rcv')  272 us
    psum x1, waiting for transfers between devices, per_device(): picked = lax.psum(ref_terms.astype(jnp.bfloat16), 'rcv')  267 us
    all_to_all x1, waiting for transfers between devices, per_device(): lax.all_to_all(relaid, 'frq', split_axis=1, concat_axis=3, tiled=True)  26.1 us
    all_to_all x1, waiting for transfers between devices, per_device(): lax.all_to_all(cross_spec, 'frq', split_axis=3, concat_axis=1, tiled=True)  21.4 us
  transfers between devices with their start and end apart: 4, of which 4 were waited for; matrix products, arithmetic and copies ran while one was open for 2% of the time, Pallas kernels for 0%

commit v1 on v0

v1 whole, which is shorter than its diff:
```python
import functools
import math

import jax
import jax.numpy as jnp
import ml_dtypes
import numpy as np
from jax import lax
from jax.experimental import pallas as pl
from jax.experimental.pallas import tpu as pltpu
from jax.sharding import PartitionSpec as P

L = 1024
LAG_FIRST = 64
LAG_HALF = 448
LAGS = 2 * LAG_HALF
NZ, NH, NK = 8, 2, 2
NX, NY = 2, 4
NF = NX * NY
CH = 4
MESH = pl.DeviceIdType.MESH
BF16 = jnp.bfloat16
F32 = jnp.float32


def lag_constants(freq_total, freq_dev):
    reach = LAG_FIRST + np.arange(LAG_HALF, dtype=np.int64)
    lags = np.concatenate([reach, L - reach])
    bins = np.arange(freq_total, dtype=np.int64) + 1
    steps = bins[:, None] * lags[None, :] % L
    angles = steps.astype(np.float32) * np.float32(2.0 * math.pi / L)
    both = np.stack([np.cos(angles), -np.sin(angles)])
    both = both.reshape(2, NF, freq_dev, LAGS).transpose(1, 0, 2, 3).reshape(2 * freq_total, LAGS)
    inverse = (both.T * np.float32(1.0 / math.sqrt(freq_total))).astype(ml_dtypes.bfloat16)
    forward = (both * np.float32(4.0 / math.sqrt(L))).astype(ml_dtypes.bfloat16)
    swap = np.zeros((256, 256), np.float32)
    for a in range(16):
        for b in range(16):
            swap[a * 16 + b, b * 16 + a] = 1.0
    return inverse, forward, swap.astype(ml_dtypes.bfloat16)


def dot(a, b):
    return jnp.dot(a, b, preferred_element_type=F32)


def dot_nt(a, b):
    return lax.dot_general(a, b, (((1,), (1,)), ((), ())), preferred_element_type=F32)


def onehot_rows(idx_ref, first, count, base):
    row = lax.broadcasted_iota(jnp.int32, (16, 256), 0)
    lane = lax.broadcasted_iota(jnp.int32, (16, 256), 1)
    out = jnp.zeros((16, 256), F32)
    for i in range(count):
        hit = (row == i) & (lane == idx_ref[first + i] - base)
        out = jnp.where(hit, 1.0, out)
    return out.astype(BF16)


def c3_kernel(
    vs_ref, rf_ref, cs_ref, ce_ref, inv_ref, fwd_ref, swap_ref, spec_hbm,
    rel_hbm, pick_hbm,
    spec, bank, ag_a, left, mix, send1, recv1, send2, recv2, series, squashed, tap, rel, ag_b,
    load_sem, out_sem,
    a1s, a1r, a2s, a2r, a3s, a3r,
    b1s, b1r, b2s, b2r, b3s, b3r,
    x1s, x1r, x2s, x2r,
):
    mr = lax.axis_index("rcv")
    mf = lax.axis_index("frq")
    mz, mh, mk = mr // 4, (mr // 2) % 2, mr % 2
    mx, my = mf // NY, mf % NY

    def rcv_of(z, h, k):
        return (z * NH + h) * NK + k

    z_peers = [(rcv_of((mz + o) % NZ, mh, mk), mf) for o in range(1, NZ)]
    h_peer = (rcv_of(mz, 1 - mh, mk), mf)
    k_peer = (rcv_of(mz, mh, 1 - mk), mf)
    f_shift = [(dx, dy) for dx in range(NX) for dy in range(NY) if dx or dy]
    f_peers = [((mx + dx) % NX) * NY + (my + dy) % NY for dx, dy in f_shift]

    barrier = pltpu.get_barrier_semaphore()
    peers = z_peers + [h_peer, k_peer] + [(mr, j) for j in f_peers]
    for peer in peers:
        pl.semaphore_signal(barrier, inc=1, device_id=peer, device_id_type=MESH)

    loads = [
        pltpu.make_async_copy(
            spec_hbm.at[pl.ds(i * 128, 128)], spec.at[pl.ds(i * 128, 128)], load_sem.at[i]
        )
        for i in range(4)
    ]
    for load in loads:
        load.start()

    def swapped(block):
        return dot(swap_ref[...], block)

    for i in range(4):
        loads[i].wait()

        def relay(n, _):
            off = pl.multiple_of(n * 16, 16)
            block = spec[pl.ds(off, 16)].reshape(256, 256)
            bank[:, pl.ds(off, 16), :] = swapped(block).astype(BF16).reshape(16, 16, 256)
            return 0

        lax.fori_loop(i * 8, i * 8 + 8, relay, 0)

    pick_v = onehot_rows(vs_ref, mr * 4, 4, mr * 256)

    def select(f, _):
        mix_rows = dot_nt(pick_v, bank[f]).astype(BF16)
        left[f, 0:16, :] = mix_rows
        return 0

    lax.fori_loop(0, 16, select, 0)
    chosen = dot(swap_ref[0:64, :], left[:, 0:16, :].reshape(256, 512)).astype(BF16)
    for c in range(CH):
        ag_a[c, mz, mh, mk] = chosen[c * 16 : c * 16 + 16]

    def remote(src, dst, ssem, rsem, dev):
        return pltpu.make_async_remote_copy(
            src_ref=src, dst_ref=dst, send_sem=ssem, recv_sem=rsem,
            device_id=dev, device_id_type=MESH,
        )

    class Gather:
        def __init__(self, view, sems):
            s1, r1, s2, r2, s3, r3 = sems
            one = view(mz, mh, mk)
            self.first = remote(one, one, s1, r1, h_peer)
            two = view(mz, slice(None), mk)
            self.second = [
                remote(two, two, s2.at[o], r2.at[o], z_peers[o]) for o in range(NZ - 1)
            ]
            half = view(slice(None), slice(None), mk)
            self.third = remote(half, half, s3, r3, k_peer)

        def start2(self):
            self.first.wait_recv()
            for copy in self.second:
                copy.start()

        def start3(self):
            for copy in self.second:
                copy.wait_recv()
            self.third.start()

        def finish(self):
            self.first.wait_send()
            for copy in self.second:
                copy.wait_send()
            self.third.wait_send()

    def gather_a(c):
        return Gather(
            lambda z, h, k: ag_a.at[c, z, h, k],
            (a1s.at[c], a1r.at[c], a2s.at[c], a2r.at[c], a3s.at[c], a3r.at[c]),
        )

    def gather_b(c):
        return Gather(
            lambda z, h, k: ag_b.at[z, h, k, :, pl.ds(c * 1024, 1024)],
            (b1s.at[c], b1r.at[c], b2s.at[c], b2r.at[c], b3s.at[c], b3r.at[c]),
        )

    ga = [gather_a(c) for c in range(CH)]
    gb = [gather_b(c) for c in range(CH)]

    pl.semaphore_wait(barrier, len(peers))
    for c in range(CH):
        ga[c].first.start()
    ga[0].start2()

    reach = LAG_FIRST + lax.broadcasted_iota(jnp.int32, (LAG_HALF, 128), 0)
    first, last = cs_ref[...], ce_ref[...]
    inside = (reach >= first) & (reach < last)
    span = (last - first).astype(F32)
    sine = jnp.sin(math.pi * ((reach - first).astype(F32) + 0.5) / span)
    weights = jnp.where(inside, sine * sine, 0.0)
    weights = pltpu.roll(weights, (128 - 16 * mf) % 128, 1)
    for v in range(16):
        tap[v] = jnp.broadcast_to(weights[:, v : v + 1], (LAG_HALF, 128))

    def exchange(c, src, dst, ssem, rsem):
        return [
            remote(src(c, f_peers[i]), dst(c, mf), ssem.at[c, i], rsem.at[c, i], (mr, f_peers[i]))
            for i in range(NF - 1)
        ]

    def rows(j):
        return pl.ds(pl.multiple_of(j * 32, 32), 32)

    def quad(j):
        return pl.ds(pl.multiple_of(j * 4, 4), 4)

    ex1 = [
        exchange(
            c,
            lambda c, j: send1.at[c, quad(j)],
            lambda c, j: recv1.at[c, :, rows(j), :],
            x1s, x1r,
        )
        for c in range(CH)
    ]
    ex2 = [
        exchange(
            c,
            lambda c, j: send2.at[c, :, rows(j), :],
            lambda c, j: recv2.at[c, quad(j)],
            x2s, x2r,
        )
        for c in range(CH)
    ]

    def cross_step(c):
        for g in range(2):
            block = swapped(ag_a[c, g * 4 : g * 4 + 4].reshape(256, 512))
            plain = block.astype(BF16).reshape(16, 16, 512)
            minus = (-block).astype(BF16).reshape(16, 16, 512)
            left[:, g * 16 : g * 16 + 16, :] = plain
            left[:, 32 + g * 16 : 48 + g * 16, 0:256] = minus[:, :, 256:512]
            left[:, 32 + g * 16 : 48 + g * 16, 256:512] = plain[:, :, 0:256]

        def one_bin(f, _):
            out = (dot(left[f], bank[f]) * 0.0625).astype(BF16)
            off = pl.multiple_of(f * 16, 16)
            mix[:, pl.ds(off, 16), :] = out.reshape(4, 16, 256)
            return 0

        lax.fori_loop(0, 16, one_bin, 0)
        for part in range(2):
            for g in range(2):
                block = swapped(mix[part * 2 + g]).astype(BF16)
                send1[c, g * 16 : g * 16 + 16, part * 16 : part * 16 + 16, :] = block.reshape(
                    16, 16, 256
                )
        for copy in ex1[c]:
            copy.start()
        recv1[c, :, rows(mf), :] = send1[c, quad(mf)]

    def lag_step(c):
        for copy in ex1[c]:
            copy.wait_recv()

        def one_source(q, _):
            series[...] = dot(inv_ref[...], recv1[c, q])
            for n in range(7):
                w = tap[q * 4 + c, n * 64 : n * 64 + 64, :]
                w = jnp.concatenate([w, w], axis=1)
                for h in range(2):
                    at = h * LAG_HALF + n * 64
                    x = series[at : at + 64, :] * w
                    squashed[at : at + 64, :] = (x * lax.rsqrt(1.0 + x * x)).astype(BF16)
            send2[c, q] = dot(fwd_ref[...], squashed[...]).astype(BF16)
            return 0

        lax.fori_loop(0, 4, one_source, 0)
        for copy in ex2[c]:
            copy.start()
        recv2[c, quad(mf)] = send2[c, :, rows(mf), :]

    pick_p = onehot_rows(rf_ref, mr * 8, 8, mr * 256)
    outs = []

    def turn_step(c):
        for copy in ex2[c]:
            copy.wait_recv()
        for part in range(2):
            for g in range(2):
                block = recv2[c, g * 16 : g * 16 + 16, part * 16 : part * 16 + 16, :]
                block = swapped(block.reshape(256, 256)).astype(BF16).reshape(16, 16, 256)
                at = c * 64 + part * 32 + g * 16
                rel[:, at : at + 16, :] = block
        out = pltpu.make_async_copy(
            rel.at[:, pl.ds(c * 64, 64), :], rel_hbm.at[:, pl.ds(c * 64, 64), :], out_sem.at[c]
        )
        out.start()
        outs.append(out)
        for n in range(4):
            block = rel[n * 4 : n * 4 + 4, c * 64 : c * 64 + 64, :].reshape(256, 256)
            got = dot_nt(pick_p, block)[0:8].astype(BF16)
            ag_b[mz, mh, mk, :, c * 1024 + n * 256 : c * 1024 + n * 256 + 256] = got
        gb[c].first.start()

    def head(c):
        ga[c].start3()
        if c + 1 < CH:
            ga[c + 1].start2()
        ga[c].third.wait_recv()
        cross_step(c)

    def land(c):
        gb[c].third.wait_recv()
        out = pltpu.make_async_copy(
            ag_b.at[:, :, :, :, pl.ds(c * 1024, 1024)],
            pick_hbm.at[:, :, :, :, pl.ds(c * 1024, 1024)],
            out_sem.at[CH + c],
        )
        out.start()
        outs.append(out)

    head(0)
    head(1)
    lag_step(0)
    head(2)
    lag_step(1)
    head(3)
    lag_step(2)
    turn_step(0)
    lag_step(3)
    gb[0].start2()
    turn_step(1)
    gb[0].start3()
    gb[1].start2()
    turn_step(2)
    land(0)
    gb[1].start3()
    gb[2].start2()
    turn_step(3)
    land(1)
    gb[2].start3()
    gb[3].start2()
    land(2)
    gb[3].start3()
    land(3)

    for c in range(CH):
        ga[c].finish()
        gb[c].finish()
        for copy in ex1[c] + ex2[c]:
            copy.wait_send()
    for out in outs:
        out.wait()


def final_kernel(scale, p0, p1, p2, p3, rel_ref, out_ref, right):
    @pl.when(pl.program_id(0) == 0)
    def _():
        right[...] = jnp.zeros_like(right)

    lhs = jnp.concatenate([p0[...], p1[...], p2[...], p3[...]], axis=1)
    for b in range(2):
        for c in range(CH):
            real = rel_ref[b, c * 64 : c * 64 + 32, :]
            imag = rel_ref[b, c * 64 + 32 : c * 64 + 64, :]
            at = c * 128 + b * 64
            right[b, at : at + 32, 0:256] = real
            right[b, at + 32 : at + 64, 0:256] = imag
            right[b, at : at + 32, 256:512] = imag
            right[b, at + 32 : at + 64, 256:512] = -real
        out = dot(lhs, right[b]) * scale
        out_ref[0, b] = out[:, 0:256]
        out_ref[1, b] = out[:, 256:512]


def per_device(spectra, virtual_sources, references, coda_start, coda_end):
    windows, freq_dev, rcv_dev = spectra.shape[1:]
    sources = virtual_sources.shape[0]
    picks = references.shape[0]
    inverse, forward, swap = lag_constants(freq_dev * NF, freq_dev)
    vmem = pl.BlockSpec(memory_space=pltpu.VMEM)
    smem = pl.BlockSpec(memory_space=pltpu.SMEM)
    hbm = pl.BlockSpec(memory_space=pl.ANY)
    dma = pltpu.SemaphoreType.DMA
    gather_sems = [dma((CH,))] * 2 + [dma((CH, NZ - 1))] * 2 + [dma((CH,))] * 2
    rel, picked = pl.pallas_call(
        c3_kernel,
        out_shape=(
            jax.ShapeDtypeStruct((16, 256, 256), BF16),
            jax.ShapeDtypeStruct((NZ, NH, NK, 8, 4096), BF16),
        ),
        in_specs=[smem, smem, vmem, vmem, vmem, vmem, vmem, hbm],
        out_specs=(hbm, hbm),
        scratch_shapes=[
            pltpu.VMEM((512, 16, 256), BF16),
            pltpu.VMEM((16, 512, 256), BF16),
            pltpu.VMEM((CH, NZ, NH, NK, 16, 512), BF16),
            pltpu.VMEM((16, 64, 512), BF16),
            pltpu.VMEM((4, 256, 256), BF16),
            pltpu.VMEM((CH, 32, 32, 256), BF16),
            pltpu.VMEM((CH, 4, 256, 256), BF16),
            pltpu.VMEM((CH, 4, 256, 256), BF16),
            pltpu.VMEM((CH, 32, 32, 256), BF16),
            pltpu.VMEM((LAGS, 256), F32),
            pltpu.VMEM((LAGS, 256), BF16),
            pltpu.VMEM((16, LAG_HALF, 128), F32),
            pltpu.VMEM((16, 256, 256), BF16),
            pltpu.VMEM((NZ, NH, NK, 8, 4096), BF16),
            dma((4,)),
            dma((2 * CH,)),
        ]
        + gather_sems
        + gather_sems
        + [dma((CH, NF - 1))] * 4,
        compiler_params=pltpu.CompilerParams(
            collective_id=0, has_side_effects=True, vmem_limit_bytes=56 << 20
        ),
        name="c3_exchange",
    )(
        virtual_sources,
        references,
        coda_start.reshape(1, sources),
        coda_end.reshape(1, sources),
        jnp.asarray(inverse),
        jnp.asarray(forward),
        jnp.asarray(swap),
        spectra.reshape(2 * windows, freq_dev, rcv_dev),
    )
    picked = picked.reshape(picks, 4096)
    lane_block = lambda c: pl.BlockSpec((256, 128), lambda n: (0, c * 8 + n))
    return pl.pallas_call(
        functools.partial(final_kernel, 1.0 / math.sqrt(sources)),
        grid=(8,),
        out_shape=jax.ShapeDtypeStruct((2, freq_dev, picks, rcv_dev), F32),
        in_specs=[lane_block(c) for c in range(CH)]
        + [pl.BlockSpec((2, 256, 256), lambda n: (n, 0, 0))],
        out_specs=pl.BlockSpec((2, 2, 256, 256), lambda n: (0, n, 0, 0)),
        scratch_shapes=[pltpu.VMEM((2, 512, 512), BF16)],
        compiler_params=pltpu.CompilerParams(vmem_limit_bytes=32 << 20),
        name="recorrelate",
    )(picked, picked, picked, picked, rel)


def solution(mesh):
    return jax.shard_map(
        per_device,
        mesh=mesh,
        in_specs=(P(None, None, "frq", "rcv"), P(), P(), P(), P()),
        out_specs=P(None, "frq", None, "rcv"),
        check_vma=False,
    )
```

time: 710 us -> 128 us (0.18); the launches traced: 701 us -> 127 us
  waiting for transfers between devices: 586 us -> 0 us
  Pallas kernels: 0 us -> 124 us
  local copies, waits for them, and re-layouts: 54.1 us -> 3.17 us
  matrix products: 28.4 us -> 0 us
  between operations: 14.1 us -> 0.02 us
  other arithmetic: 9.79 us -> 0 us
  starting transfers between devices: 8.31 us -> 0 us
    psum x2 -> x0, waiting for transfers between devices: 539 us -> none  [the longest x1 272 us: per_device(): sources = lax.psum(selected.astype(jnp.bfloat16), 'rcv')]
    pallas_call x0 -> x2, Pallas kernels: none -> 124 us  [the longest x1 117 us: per_device(): pl.pallas_call(c3_kernel, out_shape=(jax.ShapeDtypeStruct((16, 256, 256),...]
    all_to_all x2 -> x0, waiting for transfers between devices: 47.5 us -> none  [the longest x1 26.1 us: per_device(): lax.all_to_all(relaid, 'frq', split_axis=1, concat_axis=3, tiled=True)]
    dot_general x14 -> x0, matrix products: 28.4 us -> none  [the longest x4 12.2 us: recompress(): series = jnp.dot(inverse, flattened, preferred_element_type=jnp.float32)]
    reshape x3 -> x0, local copies, waits for them, and re-layouts: 17.8 us -> none  [the longest x1 10.7 us: recompress(): flattened = spectra_block.reshape(2 * freq_count, src_count * rcv_count)]
    convert_element_type x6 -> x0, local copies, waits for them, and re-layouts: 11.1 us -> none  [the longest x4 4.78 us: recompress(): squashed = (shaped / jnp.sqrt(1.0 + shaped * shaped)).astype(jnp.bfloat16)]
    all_to_all x2 -> x0, starting transfers between devices: 8.27 us -> none  [the longest x1 4.5 us: per_device(): lax.all_to_all(cross_spec, 'frq', split_axis=3, concat_axis=1, tiled=True)]
    squeeze x5 -> x0, local copies, waits for them, and re-layouts: 7.18 us -> none  [the longest x1 2.29 us: cross_spectra(): right_real = jnp.concatenate([spectra_block[0], spectra_block[1]], axis=0)]
  transfers between devices with their start and end apart: 4 -> 0, of which waited for: 4 -> 0; matrix products, arithmetic and copies ran while one was open for 2% -> 0% of each run, Pallas kernels for 0% -> 0%
where the time goes in v1:
time: 128 us; the launch traced here: 127 us
  Pallas kernels  124 us (97%)
  local copies, waits for them, and re-layouts  3.17 us (2%)
    pallas_call x1, Pallas kernels, per_device(): pl.pallas_call(c3_kernel, out_shape=(jax.ShapeDtypeStruct((16, 256, 256),...  117 us
    pallas_call x1, Pallas kernels, per_device(): pl.pallas_call(functools.partial(final_kernel, 1.0 / math.sqrt(sources)),...  6.63 us
    unnamed x4, local copies, waits for them, and re-layouts  3.17 us

profile of v1, /device:TPU:1, one launch (start us, length us, event | category | flops | bytes accessed | tf_op | source)
XLA Modules:
  0.0 126.8 jit_solution(17984828157682702906)
XLA Ops:
  0.0 116.9 %c3_exchange.1 = (bf16[16,256,256]{2,1,0:T(8,128)(2,1)}, bf16[8,2,2,8,4096]{4,3,2,1,0:T(8,128)(2,1)}) custom-call(s32[128]{0:T(128)} %vs_ref.1, s32[256]{0:T(256)} %rf_ref.1, s32[1,128]{1,0:T(1,128)} %bitcast.9, s32[1,128]{1,0:T(1,128)} %bitcast.10, bf16[896,256]{1,0:T(8,128)(2,1)} %constant.6.clone.inv_ref, bf16[256,896]{1,0:T(8,128)(2,1)} %constant.7.clone.fwd_ref, ...), custom_call_target="tpu_custom_call" | custom-call | tf_op jit(solution)/shard_map/c3_exchange/pallas_call | solution.py:370
  117.0 0.0 copy-start
  117.0 1.6 %copy-done = bf16[8,2,2,8,4096]{4,3,2,1,0:T(8,128)(2,1)S(1)} copy-done((bf16[8,2,2,8,4096]{4,3,2,1,0:T(8,128)(2,1)S(1)}, bf16[8,2,2,8,4096]{4,3,2,1,0:T(8,128)(2,1)}, u32[]{:S(2)}) %copy-start) | copy-done | bytes 2097176
  118.5 0.0 copy-start.1
  118.6 1.6 %copy-done.1 = bf16[16,256,256]{2,1,0:T(8,128)(2,1)S(1)} copy-done((bf16[16,256,256]{2,1,0:T(8,128)(2,1)S(1)}, bf16[16,256,256]{2,1,0:T(8,128)(2,1)}, u32[]{:S(2)}) %copy-start.1) | copy-done | bytes 2097176
  120.1 6.6 %recorrelate.1 = f32[2,16,256,256]{3,2,1,0:T(8,128)} custom-call(bf16[256,4096]{1,0:T(8,128)(2,1)S(1)} %bitcast.4, bf16[256,4096]{1,0:T(8,128)(2,1)S(1)} %bitcast.5, bf16[256,4096]{1,0:T(8,128)(2,1)S(1)} %bitcast.6, bf16[256,4096]{1,0:T(8,128)(2,1)S(1)} %bitcast.7, bf16[16,256,256]{2,1,0:T(8,128)(2,1)S(1)} %copy-done.1), custom_call_target="tpu_custom_call" | custom-call | tf_op jit(solution)/shard_map/recorrelate/pallas_call | solution.py:415
Async XLA Ops:
  117.0 1.6 %copy-start = (bf16[8,2,2,8,4096]{4,3,2,1,0:T(8,128)(2,1)S(1)}, bf16[8,2,2,8,4096]{4,3,2,1,0:T(8,128)(2,1)}, u32[]{:S(2)}) copy-start(bf16[8,2,2,8,4096]{4,3,2,1,0:T(8,128)(2,1)} %get-tuple-element.7) | copy-start | bytes 6291460
  118.5 1.6 %copy-start.1 = (bf16[16,256,256]{2,1,0:T(8,128)(2,1)S(1)}, bf16[16,256,256]{2,1,0:T(8,128)(2,1)}, u32[]{:S(2)}) copy-start(bf16[16,256,256]{2,1,0:T(8,128)(2,1)} %get-tuple-element.8.rel_ref) | copy-start | bytes 6291460

commit v2 on v1

v2 whole, which is shorter than its diff:
```python
import functools
import math

import jax
import jax.numpy as jnp
import ml_dtypes
import numpy as np
from jax import lax
from jax.experimental import pallas as pl
from jax.experimental.pallas import tpu as pltpu
from jax.sharding import PartitionSpec as P

L = 1024
LAG_FIRST = 64
LAG_HALF = 448
LAGS = 2 * LAG_HALF
NZ, NH, NK = 8, 2, 2
NX, NY = 2, 4
NF = NX * NY
FINAL_BINS = 8
CH = 4
DEPTH = 8
MESH = pl.DeviceIdType.MESH
BF16 = jnp.bfloat16
F32 = jnp.float32


def lag_constants(freq_total, freq_dev):
    reach = LAG_FIRST + np.arange(LAG_HALF, dtype=np.int64)
    lags = np.concatenate([reach, L - reach])
    bins = np.arange(freq_total, dtype=np.int64) + 1
    steps = bins[:, None] * lags[None, :] % L
    angles = steps.astype(np.float32) * np.float32(2.0 * math.pi / L)
    both = np.stack([np.cos(angles), -np.sin(angles)])
    both = both.reshape(2, NF, 2, freq_dev // 2, LAGS).transpose(1, 2, 0, 3, 4)
    both = both.reshape(2 * freq_total, LAGS)
    inverse = (both.T * np.float32(1.0 / math.sqrt(freq_total))).astype(ml_dtypes.bfloat16)
    forward = (both * np.float32(4.0 / math.sqrt(L))).astype(ml_dtypes.bfloat16)
    swap = np.zeros((256, 256), np.float32)
    for a in range(16):
        for b in range(16):
            swap[a * 16 + b, b * 16 + a] = 1.0
    piece = np.zeros((128, 512), np.float32)
    for v in range(4):
        for f in range(16):
            for part in range(2):
                piece[(v * 16 + f) * 2 + part, part * 256 + f * 16 + v] = 1.0
    return inverse, forward, swap.astype(ml_dtypes.bfloat16), piece.astype(ml_dtypes.bfloat16)


def dot(a, b):
    return jnp.dot(a, b, preferred_element_type=F32)


def dot_nt(a, b):
    return lax.dot_general(a, b, (((1,), (1,)), ((), ())), preferred_element_type=F32)


def onehot_rows(idx_ref, first, count, base):
    row = lax.broadcasted_iota(jnp.int32, (16, 256), 0)
    lane = lax.broadcasted_iota(jnp.int32, (16, 256), 1)
    out = jnp.zeros((16, 256), F32)
    for i in range(count):
        hit = (row == i) & (lane == idx_ref[first + i] - base)
        out = jnp.where(hit, 1.0, out)
    return out.astype(BF16)


def c3_kernel(
    vs_ref, rf_ref, cs_ref, ce_ref, inv_hbm, fwd_hbm, swap_ref, piece_ref, spec_hbm,
    rel_hbm, pick_hbm,
    spec, bank, ag_a, left, mix, send1, recv1, send2, recv2, series, squashed, tap, rel, ag_b,
    inv_ref, fwd_ref, load_sem, out_sem,
    a1s, a1r, a2s, a2r, a3s, a3r,
    d1s, d1r, d2s, d2r,
    x1s, x1r, x2s, x2r,
):
    mr = lax.axis_index("rcv")
    mf = lax.axis_index("frq")
    mz, mh, mk = mr // 4, (mr // 2) % 2, mr % 2
    mx, my = mf // NY, mf % NY

    def rcv_of(z, h, k):
        return (z * NH + h) * NK + k

    plane_peers = [
        (rcv_of((mz + o) % NZ, (mh + p) % NH, mk), mf)
        for p in range(NH)
        for o in (4, 3, 5, 2, 6, 1, 7, 0)
        if o or p
    ]
    h_peer = (rcv_of(mz, 1 - mh, mk), mf)
    k_peer = (rcv_of(mz, mh, 1 - mk), mf)
    f_shift = [(dx, dy) for dx in range(NX) for dy in range(NY) if dx or dy]
    f_peers = [((mx + dx) % NX) * NY + (my + dy) % NY for dx, dy in f_shift]

    barrier = pltpu.get_barrier_semaphore()
    peers = plane_peers + [k_peer] + [(mr, j) for j in f_peers]
    for peer in peers:
        pl.semaphore_signal(barrier, inc=1, device_id=peer, device_id_type=MESH)

    loads = [
        pltpu.make_async_copy(
            spec_hbm.at[pl.ds(i * 64, 64)], spec.at[pl.ds(i * 64, 64)], load_sem.at[i]
        )
        for i in range(8)
    ]
    tables = [
        pltpu.make_async_copy(inv_hbm, inv_ref, load_sem.at[8]),
        pltpu.make_async_copy(fwd_hbm, fwd_ref, load_sem.at[9]),
    ]
    for load in loads + tables:
        load.start()

    def swapped(block):
        return dot(swap_ref[...], block)

    for i in range(8):
        loads[i].wait()

        def relay(n, _):
            off = pl.multiple_of(n * 16, 16)
            block = spec[pl.ds(off, 16)].reshape(256, 256)
            bank[:, pl.ds(off, 16), :] = swapped(block).astype(BF16).reshape(16, 16, 256)
            return 0

        lax.fori_loop(i * 4, i * 4 + 4, relay, 0, unroll=4)

    pick_v = onehot_rows(vs_ref, mr * 4, 4, mr * 256)

    def select(f, _):
        mix_rows = dot_nt(pick_v, bank[f]).astype(BF16)
        left[f, 0:16, :] = mix_rows
        return 0

    lax.fori_loop(0, 16, select, 0, unroll=4)
    chosen = jnp.concatenate(
        [left[:, 0:16, 0:256].reshape(256, 256), left[:, 0:16, 256:512].reshape(256, 256)], axis=0
    )
    chosen = dot(piece_ref[...], chosen).astype(BF16)
    for c in range(CH):
        for half in range(2):
            at = c * 32 + half * 16
            ag_a[c, half, mz, mh, mk] = chosen[at : at + 16]

    def remote(src, dst, ssem, rsem, dev):
        return pltpu.make_async_remote_copy(
            src_ref=src, dst_ref=dst, send_sem=ssem, recv_sem=rsem,
            device_id=dev, device_id_type=MESH,
        )

    def z_peer(o):
        return rcv_of((mz + o) % NZ, mh, mk), mf

    class Gather:
        def __init__(self, view, sems):
            s1, r1, s2, r2, s3, r3 = sems
            one = view(mz, mh, mk)
            self.first = remote(one, one, s1, r1, h_peer)
            two = view(mz, slice(None), mk)
            self.near = [
                remote(two, two, s2.at[i], r2.at[i], z_peer(o))
                for i, o in enumerate((2, -2, 1, -1))
            ]
            self.far = []
            for i, o in enumerate((1, -1)):
                two = view((mz - 2 * o) % NZ, slice(None), mk)
                one = view((mz - 2 * o) % NZ, i, mk)
                self.far.append(
                    [
                        remote(two, two, s2.at[4 + i], r2.at[4 + i], z_peer(o)),
                        remote(one, one, s2.at[6 + i], r2.at[6 + i], z_peer(2 * o)),
                    ]
                )
            half = view(slice(None), slice(None), mk)
            self.third = remote(half, half, s3, r3, k_peer)

        def start1(self):
            self.first.wait_recv()
            for copy in self.near:
                copy.start()

        def start2(self):
            for i in range(2):
                self.near[i].wait_recv()
                for copy in self.far[i]:
                    copy.start()

        def start3(self):
            for copy in self.near[2:] + self.far[0] + self.far[1]:
                copy.wait_recv()
            self.third.start()

        def finish(self):
            self.first.wait_send()
            for copy in self.near + self.far[0] + self.far[1]:
                copy.wait_send()
            self.third.wait_send()

    class Direct:
        def __init__(self, view, sems, out_view=None, out_sem=None):
            s1, r1, s3, r3 = sems
            one = view(mz, mh, mk)
            self.near = [
                remote(one, one, s1.at[i], r1.at[i], peer) for i, peer in enumerate(plane_peers)
            ]
            half = view(slice(None), slice(None), mk)
            landing = half if out_view is None else out_view(slice(None), slice(None), mk)
            self.third = remote(half, landing, s3, r3, k_peer)
            self.local = None
            if out_view is not None:
                self.local = pltpu.make_async_copy(half, landing, out_sem)

        def start1(self):
            for copy in self.near:
                copy.start()

        def start3(self):
            for copy in self.near:
                copy.wait_recv()
            self.third.start()
            if self.local is not None:
                self.local.start()

        def finish(self):
            for copy in self.near:
                copy.wait_send()
            self.third.wait_send()
            if self.local is not None:
                self.third.wait_recv()
                self.local.wait()

    def pair_sems(c, s1, r1, s2, r2, s3, r3):
        return s1.at[c], r1.at[c], s2.at[c], r2.at[c], s3.at[c], r3.at[c]

    da = [
        Direct(
            lambda z, h, k, half=half: ag_a.at[0, half, z, h, k],
            (d1s.at[half], d1r.at[half], d2s.at[half], d2r.at[half]),
        )
        for half in range(2)
    ]
    ga = [None] + [
        Gather(
            lambda z, h, k, c=c: ag_a.at[c, :, z, h, k],
            pair_sems(c - 1, a1s, a1r, a2s, a2r, a3s, a3r),
        )
        for c in range(1, CH)
    ]
    def pick_gather(n, first, count):
        return Direct(
            lambda z, h, k: ag_b.at[z, h, k, :, pl.ds(first, count)],
            (d1s.at[2 + n], d1r.at[2 + n], d2s.at[2 + n], d2r.at[2 + n]),
            lambda z, h, k: pick_hbm.at[z, h, k, :, pl.ds(first, count)],
            out_sem.at[2, n],
        )

    db = [pick_gather(c, c * 1024, 1024) for c in range(CH - 1)]
    db = db + [pick_gather(CH - 1 + half, 3072 + half * 512, 512) for half in range(2)]

    pl.semaphore_wait(barrier, len(peers))
    da[0].start1()
    for c in range(1, CH):
        ga[c].first.start()

    reach = LAG_FIRST + lax.broadcasted_iota(jnp.int32, (LAG_HALF, 128), 0)
    first, last = cs_ref[...], ce_ref[...]
    inside = (reach >= first) & (reach < last)
    span = (last - first).astype(F32)
    sine = jnp.sin(math.pi * ((reach - first).astype(F32) + 0.5) / span)
    weights = jnp.where(inside, sine * sine, 0.0)
    weights = pltpu.roll(weights, (128 - 16 * mf) % 128, 1)
    for v in range(16):
        tap[v] = jnp.broadcast_to(weights[:, v : v + 1], (LAG_HALF, 128))
    da[1].start1()

    def rows(j):
        return pl.ds(pl.multiple_of(j * 32, 32), 32)

    def part_rows(j, half):
        return pl.ds(pl.multiple_of(j * 32 + half * 16, 16), 16)

    def quad(j):
        return pl.ds(pl.multiple_of(j * 4, 4), 4)

    def exchange(n, src, dst, ssem, rsem):
        return [
            remote(src(j), dst(mf), ssem.at[n, i], rsem.at[n, i], (mr, j))
            for i, j in enumerate(f_peers)
        ]

    ex1 = [
        exchange(
            half,
            lambda j, half=half: send1.at[0, quad(j), pl.ds(half * 16, 16), :],
            lambda j, half=half: recv1.at[0, :, part_rows(j, half), :],
            x1s, x1r,
        )
        for half in range(2)
    ] + [
        exchange(
            c + 1,
            lambda j, c=c: send1.at[c, quad(j)],
            lambda j, c=c: recv1.at[c, :, rows(j), :],
            x1s, x1r,
        )
        for c in range(1, CH)
    ]
    ex2 = [
        exchange(
            c,
            lambda j, c=c: send2.at[c, :, rows(j), :],
            lambda j, c=c: recv2.at[c, quad(j)],
            x2s, x2r,
        )
        for c in range(CH - 1)
    ] + [
        exchange(
            3 + half,
            lambda j, half=half: send2.at[3, :, part_rows(j, half), :],
            lambda j, half=half: recv2.at[3, quad(j), pl.ds(half * 16, 16), :],
            x2s, x2r,
        )
        for half in range(2)
    ]
    issued = []

    def send(group):
        if len(issued) >= DEPTH:
            for copy in issued[-DEPTH]:
                copy.wait_send()
        for copy in group:
            copy.start()
        issued.append(group)

    def cross_half(c, half):
        first = half * 8
        for g in range(2):
            block = swapped(ag_a[c, half, g * 4 : g * 4 + 4].reshape(256, 256))
            plain = block.astype(BF16).reshape(8, 2, 16, 256)
            minus = (-block).astype(BF16).reshape(8, 2, 16, 256)
            at = g * 16
            left[first : first + 8, at : at + 16, 0:256] = plain[:, 0]
            left[first : first + 8, at : at + 16, 256:512] = plain[:, 1]
            left[first : first + 8, 32 + at : 48 + at, 0:256] = minus[:, 1]
            left[first : first + 8, 32 + at : 48 + at, 256:512] = plain[:, 0]

        def one_bin(f, _):
            out = (dot(left[first + f], bank[first + f]) * 0.0625).astype(BF16)
            out = out.reshape(4, 16, 256)
            for part in range(2):
                off = pl.multiple_of(part * 128 + f * 16, 16)
                mix[half, :, pl.ds(off, 16), :] = out[part * 2 : part * 2 + 2]
            return 0

        lax.fori_loop(0, 8, one_bin, 0, unroll=4)
        for g in range(2):
            block = swapped(mix[half, g]).astype(BF16)
            send1[c, g * 16 : g * 16 + 16, half * 16 : half * 16 + 16, :] = block.reshape(
                16, 16, 256
            )

    def cross_first(half):
        da[half].third.wait_recv()
        cross_half(0, half)
        send(ex1[half])
        recv1[0, :, part_rows(mf, half), :] = send1[0, quad(mf), half * 16 : half * 16 + 16, :]

    def cross(c):
        ga[c].third.wait_recv()
        cross_half(c, 0)
        cross_half(c, 1)
        send(ex1[c + 1])
        recv1[c, :, rows(mf), :] = send1[c, quad(mf)]

    def lag_step(c):
        for copy in ex1[0] + ex1[1] if c == 0 else ex1[c + 1]:
            copy.wait_recv()

        def two_sources(pair, _):
            for i in range(2):
                q = pair * 2 + i
                series[i] = dot(inv_ref[...], recv1[c, q])
                for n in range(7):
                    w = tap[q * 4 + c, n * 64 : n * 64 + 64, :]
                    w = jnp.concatenate([w, w], axis=1)
                    for h in range(2):
                        at = h * LAG_HALF + n * 64
                        x = series[i, at : at + 64, :] * w
                        squashed[i, at : at + 64, :] = (x * lax.rsqrt(1.0 + x * x)).astype(BF16)
                send2[c, q] = dot(fwd_ref[...], squashed[i]).astype(BF16)
            return 0

        lax.fori_loop(0, 2, two_sources, 0)
        send(ex2[c])
        if c == CH - 1:
            send(ex2[CH])
        recv2[c, quad(mf)] = send2[c, :, rows(mf), :]

    pick_p = onehot_rows(rf_ref, mr * 8, 8, mr * 256)
    outs = []

    def turn_half(c, half):
        first = half * 8
        for g in range(2):
            block = recv2[c, g * 16 : g * 16 + 16, half * 16 : half * 16 + 16, :]
            block = swapped(block.reshape(256, 256)).astype(BF16).reshape(2, 8, 16, 256)
            for part in range(2):
                at = c * 64 + part * 32 + g * 16
                rel[first : first + 8, at : at + 16, :] = block[part]
        out = pltpu.make_async_copy(
            rel.at[pl.ds(first, 8), pl.ds(c * 64, 64), :],
            rel_hbm.at[pl.ds(first, 8), pl.ds(c * 64, 64), :],
            out_sem.at[half, c],
        )
        out.start()
        outs.append(out)
        for n in range(half * 2, half * 2 + 2):
            order = (1, 0, 3, 2) if c % 2 else (0, 1, 2, 3)
            block = [rel[n * 4 + i, c * 64 : c * 64 + 64, :] for i in order]
            block = jnp.concatenate(block, axis=0)
            got = dot_nt(pick_p, block)[0:8].astype(BF16)
            ag_b[mz, mh, mk, :, c * 1024 + n * 256 : c * 1024 + n * 256 + 256] = got

    def turn_step(c):
        for copy in ex2[c]:
            copy.wait_recv()
        turn_half(c, 0)
        turn_half(c, 1)
        db[c].start1()

    def turn_last(half):
        for copy in ex2[CH - 1 + half]:
            copy.wait_recv()
        turn_half(CH - 1, half)
        db[CH - 1 + half].start1()

    da[0].start3()
    ga[1].start1()
    da[1].start3()
    cross_first(0)
    ga[1].start2()
    ga[2].start1()
    cross_first(1)
    ga[1].start3()
    ga[2].start2()
    ga[3].start1()
    cross(1)
    ga[2].start3()
    ga[3].start2()
    cross(2)
    ga[3].start3()
    for table in tables:
        table.wait()
    lag_step(0)
    cross(3)
    lag_step(1)
    lag_step(2)
    turn_step(0)
    lag_step(3)
    turn_step(1)
    turn_step(2)
    db[0].start3()
    turn_last(0)
    db[1].start3()
    turn_last(1)
    db[2].start3()
    db[3].start3()
    db[4].start3()

    for gather in ga[1:] + da + db:
        gather.finish()
    for group in issued[-DEPTH:]:
        for copy in group:
            copy.wait_send()
    for out in outs:
        out.wait()


def final_kernel(scale, p0, p1, p2, p3, rel_ref, out_ref):
    low = lax.broadcasted_iota(jnp.int32, (256, 128), 1) < 64
    for b in range(FINAL_BINS):
        odd = b % 2
        lanes = slice(b // 2 * 128, b // 2 * 128 + 128)
        pieces = [p[:, lanes] for p in (p0, p1, p2, p3)]
        left, real, imag = [], [], []
        for c in range(CH):
            if c % 2 == 0:
                left.append(jnp.where(low, pieces[c + odd], pieces[c + 1 - odd]))
            at = (c ^ odd) * 64
            one, other = rel_ref[b, at : at + 32, :], rel_ref[b, at + 32 : at + 64, :]
            real += [one, other]
            imag += [other, -one]
        left = jnp.concatenate(left, axis=1)
        out_ref[0, b] = dot(left, jnp.concatenate(real, axis=0)) * scale
        out_ref[1, b] = dot(left, jnp.concatenate(imag, axis=0)) * scale


def per_device(spectra, virtual_sources, references, coda_start, coda_end):
    windows, freq_dev, rcv_dev = spectra.shape[1:]
    sources = virtual_sources.shape[0]
    picks = references.shape[0]
    inverse, forward, swap, piece = lag_constants(freq_dev * NF, freq_dev)
    vmem = pl.BlockSpec(memory_space=pltpu.VMEM)
    smem = pl.BlockSpec(memory_space=pltpu.SMEM)
    hbm = pl.BlockSpec(memory_space=pl.ANY)
    dma = pltpu.SemaphoreType.DMA
    gather_sems = [dma((CH - 1,))] * 2 + [dma((CH - 1, 8))] * 2 + [dma((CH - 1,))] * 2
    rel, picked = pl.pallas_call(
        c3_kernel,
        out_shape=(
            jax.ShapeDtypeStruct((16, 256, 256), BF16),
            jax.ShapeDtypeStruct((NZ, NH, NK, 8, 4096), BF16),
        ),
        in_specs=[smem, smem, vmem, vmem, hbm, hbm, vmem, vmem, hbm],
        out_specs=(hbm, hbm),
        scratch_shapes=[
            pltpu.VMEM((512, 16, 256), BF16),
            pltpu.VMEM((16, 512, 256), BF16),
            pltpu.VMEM((CH, 2, NZ, NH, NK, 16, 256), BF16),
            pltpu.VMEM((16, 64, 512), BF16),
            pltpu.VMEM((2, 2, 256, 256), BF16),
            pltpu.VMEM((CH, 32, 32, 256), BF16),
            pltpu.VMEM((CH, 4, 256, 256), BF16),
            pltpu.VMEM((CH, 4, 256, 256), BF16),
            pltpu.VMEM((CH, 32, 32, 256), BF16),
            pltpu.VMEM((2, LAGS, 256), F32),
            pltpu.VMEM((2, LAGS, 256), BF16),
            pltpu.VMEM((16, LAG_HALF, 128), F32),
            pltpu.VMEM((16, 256, 256), BF16),
            pltpu.VMEM((NZ, NH, NK, 8, 4096), BF16),
            pltpu.VMEM((LAGS, 256), BF16),
            pltpu.VMEM((256, LAGS), BF16),
            dma((10,)),
            dma((3, CH + 1)),
        ]
        + gather_sems
        + [dma((CH + 3, 15))] * 2
        + [dma((CH + 3,))] * 2
        + [dma((CH + 1, NF - 1))] * 4,
        compiler_params=pltpu.CompilerParams(
            collective_id=0, has_side_effects=True, vmem_limit_bytes=56 << 20
        ),
        name="c3_exchange",
    )(
        virtual_sources,
        references,
        coda_start.reshape(1, sources),
        coda_end.reshape(1, sources),
        jnp.asarray(inverse),
        jnp.asarray(forward),
        jnp.asarray(swap),
        jnp.asarray(piece),
        spectra.reshape(2 * windows, freq_dev, rcv_dev),
    )
    picked = picked.reshape(picks, 4096)
    steps = freq_dev // FINAL_BINS
    lane_block = lambda c: pl.BlockSpec(
        (256, 64 * FINAL_BINS), lambda n: (0, c * steps + n)
    )
    return pl.pallas_call(
        functools.partial(final_kernel, 1.0 / math.sqrt(sources)),
        grid=(steps,),
        out_shape=jax.ShapeDtypeStruct((2, freq_dev, picks, rcv_dev), F32),
        in_specs=[lane_block(c) for c in range(CH)]
        + [pl.BlockSpec((FINAL_BINS, 256, 256), lambda n: (n, 0, 0))],
        out_specs=pl.BlockSpec((2, FINAL_BINS, 256, 256), lambda n: (0, n, 0, 0)),
        compiler_params=pltpu.CompilerParams(vmem_limit_bytes=60 << 20),
        name="recorrelate",
    )(picked, picked, picked, picked, rel)


def solution(mesh):
    return jax.shard_map(
        per_device,
        mesh=mesh,
        in_specs=(P(None, None, "frq", "rcv"), P(), P(), P(), P()),
        out_specs=P(None, "frq", None, "rcv"),
        check_vma=False,
    )
```

time: 128 us -> 104 us (0.81)
  Pallas kernels: 124 us -> 103 us
  local copies, waits for them, and re-layouts: 3.17 us -> 0 us
    pallas_call x1, Pallas kernels: 117 us -> 97.7 us  [per_device(): pl.pallas_call(c3_kernel, out_shape=(jax.ShapeDtypeStruct((16, 256, 256),...]
    unnamed x4 -> x0, local copies, waits for them, and re-layouts: 3.17 us -> none
where the time goes in v2:
time: 104 us; the launch traced here: 103 us
  Pallas kernels  103 us (99%)
    pallas_call x1, Pallas kernels, per_device(): pl.pallas_call(c3_kernel, out_shape=(jax.ShapeDtypeStruct((16, 256, 256),...  97.7 us
    pallas_call x1, Pallas kernels, per_device(): pl.pallas_call(functools.partial(final_kernel, 1.0 / math.sqrt(sources)),...  5.7 us

profile of v2, /device:TPU:1, one launch (start us, length us, event | category | flops | bytes accessed | tf_op | source)
XLA Modules:
  0.0 103.4 jit_solution(4588886552820563651)
XLA Ops:
  0.0 97.7 %c3_exchange.1 = (bf16[16,256,256]{2,1,0:T(8,128)(2,1)}, bf16[8,2,2,8,4096]{4,3,2,1,0:T(8,128)(2,1)}) custom-call(s32[128]{0:T(128)} %vs_ref.1, s32[256]{0:T(256)} %rf_ref.1, s32[1,128]{1,0:T(1,128)} %bitcast.9, s32[1,128]{1,0:T(1,128)} %bitcast.10, bf16[896,256]{1,0:T(8,128)(2,1)} %constant.8.clone.inv_hbm, bf16[256,896]{1,0:T(8,128)(2,1)} %constant.9.clone.fwd_hbm, ...), custom_call_target="tpu_custom_call" | custom-call | tf_op jit(solution)/shard_map/c3_exchange/pallas_call | solution.py:509
  97.7 5.7 %recorrelate.1 = f32[2,16,256,256]{3,2,1,0:T(8,128)} custom-call(bf16[256,4096]{1,0:T(8,128)(2,1)} %bitcast.4, bf16[256,4096]{1,0:T(8,128)(2,1)} %bitcast.5, bf16[256,4096]{1,0:T(8,128)(2,1)} %bitcast.6, bf16[256,4096]{1,0:T(8,128)(2,1)} %bitcast.7, bf16[16,256,256]{2,1,0:T(8,128)(2,1)} %get-tuple-element.8.rel_ref), custom_call_target="tpu_custom_call" | custom-call | tf_op jit(solution)/shard_map/recorrelate/pallas_call | solution.py:561

commit v3 on v2

--- a/solution.py
+++ b/solution.py
@@ -19,7 +19,6 @@
 NF = NX * NY
 FINAL_BINS = 8
 CH = 4
-DEPTH = 8
 MESH = pl.DeviceIdType.MESH
 BF16 = jnp.bfloat16
 F32 = jnp.float32
@@ -67,12 +66,12 @@
 
 
 def c3_kernel(
-    vs_ref, rf_ref, cs_ref, ce_ref, inv_hbm, fwd_hbm, swap_ref, piece_ref, spec_hbm,
+    vs_ref, rf_ref, cs_ref, ce_ref, inv_hbm, fwd_hbm, swap_hbm, piece_hbm, spec_hbm,
     rel_hbm, pick_hbm,
     spec, bank, ag_a, left, mix, send1, recv1, send2, recv2, series, squashed, tap, rel, ag_b,
-    inv_ref, fwd_ref, load_sem, out_sem,
+    inv_ref, fwd_ref, swap_ref, piece_ref, load_sem, out_sem,
     a1s, a1r, a2s, a2r, a3s, a3r,
-    d1s, d1r, d2s, d2r,
+    d0s, d0r, d1s, d1r, d2s, d2r,
     x1s, x1r, x2s, x2r,
 ):
     mr = lax.axis_index("rcv")
@@ -83,19 +82,14 @@
     def rcv_of(z, h, k):
         return (z * NH + h) * NK + k
 
-    plane_peers = [
-        (rcv_of((mz + o) % NZ, (mh + p) % NH, mk), mf)
-        for p in range(NH)
-        for o in (4, 3, 5, 2, 6, 1, 7, 0)
-        if o or p
-    ]
+    z_peers = [(rcv_of((mz + o) % NZ, mh, mk), mf) for o in range(1, NZ)]
     h_peer = (rcv_of(mz, 1 - mh, mk), mf)
     k_peer = (rcv_of(mz, mh, 1 - mk), mf)
     f_shift = [(dx, dy) for dx in range(NX) for dy in range(NY) if dx or dy]
     f_peers = [((mx + dx) % NX) * NY + (my + dy) % NY for dx, dy in f_shift]
 
     barrier = pltpu.get_barrier_semaphore()
-    peers = plane_peers + [k_peer] + [(mr, j) for j in f_peers]
+    peers = z_peers + [h_peer, k_peer] + [(mr, j) for j in f_peers]
     for peer in peers:
         pl.semaphore_signal(barrier, inc=1, device_id=peer, device_id_type=MESH)
 
@@ -109,8 +103,14 @@
         pltpu.make_async_copy(inv_hbm, inv_ref, load_sem.at[8]),
         pltpu.make_async_copy(fwd_hbm, fwd_ref, load_sem.at[9]),
     ]
-    for load in loads + tables:
+    early = [
+        pltpu.make_async_copy(swap_hbm, swap_ref, load_sem.at[10]),
+        pltpu.make_async_copy(piece_hbm, piece_ref, load_sem.at[11]),
+    ]
+    for load in early + loads + tables:
         load.start()
+    for load in early:
+        load.wait()
 
     def swapped(block):
         return dot(swap_ref[...], block)
@@ -152,6 +152,23 @@
     def z_peer(o):
         return rcv_of((mz + o) % NZ, mh, mk), mf
 
+    class Group:
+        def __init__(self, copies, whole, ssem, rsem):
+            self.copies = copies
+            self.whole = whole
+            self.ssem = ssem
+            self.rsem = rsem
+
+        def start(self):
+            for copy in self.copies:
+                copy.start()
+
+        def wait_send(self):
+            pltpu.make_async_copy(self.whole, self.whole, self.ssem).wait()
+
+        def wait_recv(self):
+            pltpu.make_async_copy(self.whole, self.whole, self.rsem).wait()
+
     class Gather:
         def __init__(self, view, sems):
             s1, r1, s2, r2, s3, r3 = sems
@@ -159,7 +176,7 @@
             self.first = remote(one, one, s1, r1, h_peer)
             two = view(mz, slice(None), mk)
             self.near = [
-                remote(two, two, s2.at[i], r2.at[i], z_peer(o))
+                remote(two, two, s2, r2.at[min(i, 2)], z_peer(o))
                 for i, o in enumerate((2, -2, 1, -1))
             ]
             self.far = []
@@ -168,10 +185,12 @@
                 one = view((mz - 2 * o) % NZ, i, mk)
                 self.far.append(
                     [
-                        remote(two, two, s2.at[4 + i], r2.at[4 + i], z_peer(o)),
-                        remote(one, one, s2.at[6 + i], r2.at[6 + i], z_peer(2 * o)),
+                        remote(two, two, s2, r2.at[2], z_peer(o)),
+                        remote(one, one, s2, r2.at[2], z_peer(2 * o)),
                     ]
                 )
+            self.all_sent = Group([], view(pl.ds(0, 7), slice(None), mk), s2, s2)
+            self.rest = Group([], view(pl.ds(0, 5), slice(None), mk), s2, r2.at[2])
             half = view(slice(None), slice(None), mk)
             self.third = remote(half, half, s3, r3, k_peer)
 
@@ -187,23 +206,22 @@
                     copy.start()
 
         def start3(self):
-            for copy in self.near[2:] + self.far[0] + self.far[1]:
-                copy.wait_recv()
+            self.rest.wait_recv()
             self.third.start()
 
         def finish(self):
             self.first.wait_send()
-            for copy in self.near + self.far[0] + self.far[1]:
-                copy.wait_send()
+            self.all_sent.wait_send()
             self.third.wait_send()
 
     class Direct:
         def __init__(self, view, sems, out_view=None, out_sem=None):
-            s1, r1, s3, r3 = sems
+            s0, r0, s1, r1, s3, r3 = sems
             one = view(mz, mh, mk)
-            self.near = [
-                remote(one, one, s1.at[i], r1.at[i], peer) for i, peer in enumerate(plane_peers)
-            ]
+            self.first = remote(one, one, s0, r0, h_peer)
+            two = view(mz, slice(None), mk)
+            copies = [remote(two, two, s1, r1, z_peer(o)) for o in (4, 3, 5, 2, 6, 1, 7)]
+            self.near = Group(copies, view(pl.ds(0, NZ - 1), slice(None), mk), s1, r1)
             half = view(slice(None), slice(None), mk)
             landing = half if out_view is None else out_view(slice(None), slice(None), mk)
             self.third = remote(half, landing, s3, r3, k_peer)
@@ -212,19 +230,18 @@
                 self.local = pltpu.make_async_copy(half, landing, out_sem)
 
         def start1(self):
-            for copy in self.near:
-                copy.start()
+            self.first.wait_recv()
+            self.near.start()
 
         def start3(self):
-            for copy in self.near:
-                copy.wait_recv()
+            self.near.wait_recv()
             self.third.start()
             if self.local is not None:
                 self.local.start()
 
         def finish(self):
-            for copy in self.near:
-                copy.wait_send()
+            self.first.wait_send()
+            self.near.wait_send()
             self.third.wait_send()
             if self.local is not None:
                 self.third.wait_recv()
@@ -233,10 +250,13 @@
     def pair_sems(c, s1, r1, s2, r2, s3, r3):
         return s1.at[c], r1.at[c], s2.at[c], r2.at[c], s3.at[c], r3.at[c]
 
+    def direct_sems(n):
+        return d0s.at[n], d0r.at[n], d1s.at[n], d1r.at[n], d2s.at[n], d2r.at[n]
+
     da = [
         Direct(
             lambda z, h, k, half=half: ag_a.at[0, half, z, h, k],
-            (d1s.at[half], d1r.at[half], d2s.at[half], d2r.at[half]),
+            direct_sems(half),
         )
         for half in range(2)
     ]
@@ -250,7 +270,7 @@
     def pick_gather(n, first, count):
         return Direct(
             lambda z, h, k: ag_b.at[z, h, k, :, pl.ds(first, count)],
-            (d1s.at[2 + n], d1r.at[2 + n], d2s.at[2 + n], d2r.at[2 + n]),
+            direct_sems(2 + n),
             lambda z, h, k: pick_hbm.at[z, h, k, :, pl.ds(first, count)],
             out_sem.at[2, n],
         )
@@ -259,9 +279,9 @@
     db = db + [pick_gather(CH - 1 + half, 3072 + half * 512, 512) for half in range(2)]
 
     pl.semaphore_wait(barrier, len(peers))
+    for gather in da + ga[1:]:
+        gather.first.start()
     da[0].start1()
-    for c in range(1, CH):
-        ga[c].first.start()
 
     reach = LAG_FIRST + lax.broadcasted_iota(jnp.int32, (LAG_HALF, 128), 0)
     first, last = cs_ref[...], ce_ref[...]
@@ -283,18 +303,19 @@
     def quad(j):
         return pl.ds(pl.multiple_of(j * 4, 4), 4)
 
-    def exchange(n, src, dst, ssem, rsem):
-        return [
-            remote(src(j), dst(mf), ssem.at[n, i], rsem.at[n, i], (mr, j))
-            for i, j in enumerate(f_peers)
-        ]
+    def exchange(n, src, dst, whole, ssem, rsem):
+        copies = [remote(src(j), dst(mf), ssem.at[n], rsem.at[n], (mr, j)) for j in f_peers]
+        return [Group(copies, whole, ssem.at[n], rsem.at[n])]
+
+    whole_half = send1.at[0, pl.ds(0, 4 * (NF - 1)), pl.ds(0, 16), :]
+    whole_full = send1.at[0, pl.ds(0, 4 * (NF - 1))]
 
     ex1 = [
         exchange(
             half,
             lambda j, half=half: send1.at[0, quad(j), pl.ds(half * 16, 16), :],
             lambda j, half=half: recv1.at[0, :, part_rows(j, half), :],
-            x1s, x1r,
+            whole_half, x1s, x1r,
         )
         for half in range(2)
     ] + [
@@ -302,36 +323,33 @@
             c + 1,
             lambda j, c=c: send1.at[c, quad(j)],
             lambda j, c=c: recv1.at[c, :, rows(j), :],
-            x1s, x1r,
+            whole_full, x1s, x1r,
         )
         for c in range(1, CH)
     ]
     ex2 = [
-        exchange(
-            c,
-            lambda j, c=c: send2.at[c, :, rows(j), :],
-            lambda j, c=c: recv2.at[c, quad(j)],
-            x2s, x2r,
-        )
-        for c in range(CH - 1)
-    ] + [
-        exchange(
-            3 + half,
-            lambda j, half=half: send2.at[3, :, part_rows(j, half), :],
-            lambda j, half=half: recv2.at[3, quad(j), pl.ds(half * 16, 16), :],
-            x2s, x2r,
-        )
-        for half in range(2)
+        [
+            exchange(
+                2 * c + half,
+                lambda j, c=c, half=half: send2.at[c, :, part_rows(j, half), :],
+                lambda j, c=c, half=half: recv2.at[c, quad(j), pl.ds(half * 16, 16), :],
+                whole_half, x2s, x2r,
+            )
+            for half in range(2)
+        ]
+        for c in range(CH)
     ]
-    issued = []
 
     def send(group):
-        if len(issued) >= DEPTH:
-            for copy in issued[-DEPTH]:
-                copy.wait_send()
         for copy in group:
             copy.start()
-        issued.append(group)
+
+    def sent(group):
+        for copy in group:
+            copy.wait_send()
+
+    def give_back(c, half):
+        send(ex2[c][half])
 
     def cross_half(c, half):
         first = half * 8
@@ -392,9 +410,6 @@
             return 0
 
         lax.fori_loop(0, 2, two_sources, 0)
-        send(ex2[c])
-        if c == CH - 1:
-            send(ex2[CH])
         recv2[c, quad(mf)] = send2[c, :, rows(mf), :]
 
     pick_p = onehot_rows(rf_ref, mr * 8, 8, mr * 256)
@@ -423,22 +438,22 @@
             ag_b[mz, mh, mk, :, c * 1024 + n * 256 : c * 1024 + n * 256 + 256] = got
 
     def turn_step(c):
-        for copy in ex2[c]:
+        for copy in ex2[c][0] + ex2[c][1]:
             copy.wait_recv()
         turn_half(c, 0)
         turn_half(c, 1)
-        db[c].start1()
+        db[c].first.start()
 
     def turn_last(half):
-        for copy in ex2[CH - 1 + half]:
+        for copy in ex2[CH - 1][half]:
             copy.wait_recv()
         turn_half(CH - 1, half)
-        db[CH - 1 + half].start1()
+        db[CH - 1 + half].first.start()
 
     da[0].start3()
     ga[1].start1()
+    cross_first(0)
     da[1].start3()
-    cross_first(0)
     ga[1].start2()
     ga[2].start1()
     cross_first(1)
@@ -453,26 +468,45 @@
     for table in tables:
         table.wait()
     lag_step(0)
+    give_back(0, 0)
+    give_back(0, 1)
     cross(3)
     lag_step(1)
+    give_back(1, 0)
+    for gather in da + ga[1:]:
+        gather.finish()
+    sent(ex1[0] + ex1[1] + ex1[2] + ex1[3])
+    turn_step(0)
+    give_back(1, 1)
     lag_step(2)
-    turn_step(0)
+    give_back(2, 0)
+    sent(ex1[4] + ex2[0][0] + ex2[0][1])
+    db[0].start1()
+    turn_step(1)
+    give_back(2, 1)
     lag_step(3)
-    turn_step(1)
+    give_back(3, 0)
+    db[1].start1()
+    db[0].start3()
     turn_step(2)
-    db[0].start3()
+    give_back(3, 1)
+    sent(ex2[1][0] + ex2[1][1])
+    db[0].finish()
+    db[2].start1()
     turn_last(0)
     db[1].start3()
     turn_last(1)
+    db[3].start1()
+    db[4].start1()
+    sent(ex2[2][0] + ex2[2][1])
+    db[1].finish()
     db[2].start3()
     db[3].start3()
     db[4].start3()
 
-    for gather in ga[1:] + da + db:
-        gather.finish()
-    for group in issued[-DEPTH:]:
-        for copy in group:
-            copy.wait_send()
+    for c in range(2, CH + 1):
+        db[c].finish()
+    sent(ex2[3][0] + ex2[3][1])
     for out in outs:
         out.wait()
 
@@ -505,14 +539,14 @@
     smem = pl.BlockSpec(memory_space=pltpu.SMEM)
     hbm = pl.BlockSpec(memory_space=pl.ANY)
     dma = pltpu.SemaphoreType.DMA
-    gather_sems = [dma((CH - 1,))] * 2 + [dma((CH - 1, 8))] * 2 + [dma((CH - 1,))] * 2
+    gather_sems = [dma((CH - 1,))] * 3 + [dma((CH - 1, 3))] + [dma((CH - 1,))] * 2
     rel, picked = pl.pallas_call(
         c3_kernel,
         out_shape=(
             jax.ShapeDtypeStruct((16, 256, 256), BF16),
             jax.ShapeDtypeStruct((NZ, NH, NK, 8, 4096), BF16),
         ),
-        in_specs=[smem, smem, vmem, vmem, hbm, hbm, vmem, vmem, hbm],
+        in_specs=[smem, smem, vmem, vmem, hbm, hbm, hbm, hbm, hbm],
         out_specs=(hbm, hbm),
         scratch_shapes=[
             pltpu.VMEM((512, 16, 256), BF16),
@@ -531,13 +565,17 @@
             pltpu.VMEM((NZ, NH, NK, 8, 4096), BF16),
             pltpu.VMEM((LAGS, 256), BF16),
             pltpu.VMEM((256, LAGS), BF16),
-            dma((10,)),
+            pltpu.VMEM((256, 256), BF16),
+            pltpu.VMEM((128, 512), BF16),
+            dma((12,)),
             dma((3, CH + 1)),
         ]
         + gather_sems
-        + [dma((CH + 3, 15))] * 2
         + [dma((CH + 3,))] * 2
-        + [dma((CH + 1, NF - 1))] * 4,
+        + [dma((CH + 3,))] * 2
+        + [dma((CH + 3,))] * 2
+        + [dma((CH + 1,))] * 2
+        + [dma((2 * CH,))] * 2,
         compiler_params=pltpu.CompilerParams(
             collective_id=0, has_side_effects=True, vmem_limit_bytes=56 << 20
         ),

time: 104 us -> 98.4 us (0.946)
  Pallas kernels: 103 us -> 98.3 us
    pallas_call x1, Pallas kernels: 97.7 us -> 92.6 us  [per_device(): pl.pallas_call(c3_kernel, out_shape=(jax.ShapeDtypeStruct((16, 256, 256),...]
where the time goes in v3:
time: 98.4 us; the launch traced here: 98.3 us
  Pallas kernels  98.3 us (100%)
    pallas_call x1, Pallas kernels, per_device(): pl.pallas_call(c3_kernel, out_shape=(jax.ShapeDtypeStruct((16, 256, 256),...  92.6 us
    pallas_call x1, Pallas kernels, per_device(): pl.pallas_call(functools.partial(final_kernel, 1.0 / math.sqrt(sources)),...  5.7 us

profile of v3, /device:TPU:1, one launch (start us, length us, event | category | flops | bytes accessed | tf_op | source)
XLA Modules:
  0.0 98.3 jit_solution(2334208741869726412)
XLA Ops:
  0.0 92.6 %c3_exchange.1 = (bf16[16,256,256]{2,1,0:T(8,128)(2,1)}, bf16[8,2,2,8,4096]{4,3,2,1,0:T(8,128)(2,1)}) custom-call(s32[128]{0:T(128)} %vs_ref.1, s32[256]{0:T(256)} %rf_ref.1, s32[1,128]{1,0:T(1,128)} %bitcast.9, s32[1,128]{1,0:T(1,128)} %bitcast.10, bf16[896,256]{1,0:T(8,128)(2,1)} %constant.8.clone.inv_hbm, bf16[256,896]{1,0:T(8,128)(2,1)} %constant.9.clone.fwd_hbm, ...), custom_call_target="tpu_custom_call" | custom-call | tf_op jit(solution)/shard_map/c3_exchange/pallas_call | solution.py:543
  92.7 5.7 %recorrelate.1 = f32[2,16,256,256]{3,2,1,0:T(8,128)} custom-call(bf16[256,4096]{1,0:T(8,128)(2,1)} %bitcast.4, bf16[256,4096]{1,0:T(8,128)(2,1)} %bitcast.5, bf16[256,4096]{1,0:T(8,128)(2,1)} %bitcast.6, bf16[256,4096]{1,0:T(8,128)(2,1)} %bitcast.7, bf16[16,256,256]{2,1,0:T(8,128)(2,1)} %get-tuple-element.8.rel_ref), custom_call_target="tpu_custom_call" | custom-call | tf_op jit(solution)/shard_map/recorrelate/pallas_call | solution.py:599

commit v4 on v3

--- a/solution.py
+++ b/solution.py
@@ -82,14 +82,19 @@
     def rcv_of(z, h, k):
         return (z * NH + h) * NK + k
 
-    z_peers = [(rcv_of((mz + o) % NZ, mh, mk), mf) for o in range(1, NZ)]
+    plane_peers = [
+        (rcv_of((mz + o) % NZ, (mh + p) % NH, mk), mf)
+        for p in range(NH)
+        for o in (4, 3, 5, 2, 6, 1, 7, 0)
+        if o or p
+    ]
     h_peer = (rcv_of(mz, 1 - mh, mk), mf)
     k_peer = (rcv_of(mz, mh, 1 - mk), mf)
     f_shift = [(dx, dy) for dx in range(NX) for dy in range(NY) if dx or dy]
     f_peers = [((mx + dx) % NX) * NY + (my + dy) % NY for dx, dy in f_shift]
 
     barrier = pltpu.get_barrier_semaphore()
-    peers = z_peers + [h_peer, k_peer] + [(mr, j) for j in f_peers]
+    peers = plane_peers + [k_peer] + [(mr, j) for j in f_peers]
     for peer in peers:
         pl.semaphore_signal(barrier, inc=1, device_id=peer, device_id_type=MESH)
 
@@ -170,7 +175,7 @@
             pltpu.make_async_copy(self.whole, self.whole, self.rsem).wait()
 
     class Gather:
-        def __init__(self, view, sems):
+        def __init__(self, view, sems, out_view=None, out_sem=None):
             s1, r1, s2, r2, s3, r3 = sems
             one = view(mz, mh, mk)
             self.first = remote(one, one, s1, r1, h_peer)
@@ -192,7 +197,11 @@
             self.all_sent = Group([], view(pl.ds(0, 7), slice(None), mk), s2, s2)
             self.rest = Group([], view(pl.ds(0, 5), slice(None), mk), s2, r2.at[2])
             half = view(slice(None), slice(None), mk)
-            self.third = remote(half, half, s3, r3, k_peer)
+            landing = half if out_view is None else out_view(slice(None), slice(None), mk)
+            self.third = remote(half, landing, s3, r3, k_peer)
+            self.local = None
+            if out_view is not None:
+                self.local = pltpu.make_async_copy(half, landing, out_sem)
 
         def start1(self):
             self.first.wait_recv()
@@ -208,20 +217,31 @@
         def start3(self):
             self.rest.wait_recv()
             self.third.start()
+            if self.local is not None:
+                self.local.start()
 
         def finish(self):
             self.first.wait_send()
             self.all_sent.wait_send()
             self.third.wait_send()
+            if self.local is not None:
+                self.third.wait_recv()
+                self.local.wait()
 
     class Direct:
-        def __init__(self, view, sems, out_view=None, out_sem=None):
+        def __init__(self, view, sems, out_view=None, out_sem=None, plane=False):
             s0, r0, s1, r1, s3, r3 = sems
             one = view(mz, mh, mk)
-            self.first = remote(one, one, s0, r0, h_peer)
-            two = view(mz, slice(None), mk)
-            copies = [remote(two, two, s1, r1, z_peer(o)) for o in (4, 3, 5, 2, 6, 1, 7)]
-            self.near = Group(copies, view(pl.ds(0, NZ - 1), slice(None), mk), s1, r1)
+            if plane:
+                self.first = None
+                copies = [remote(one, one, s1, r1, peer) for peer in plane_peers]
+                whole = send1.at[0, pl.ds(0, len(copies)), pl.ds(0, 16), :]
+            else:
+                self.first = remote(one, one, s0, r0, h_peer)
+                two = view(mz, slice(None), mk)
+                copies = [remote(two, two, s1, r1, z_peer(o)) for o in (4, 3, 5, 2, 6, 1, 7)]
+                whole = view(pl.ds(0, NZ - 1), slice(None), mk)
+            self.near = Group(copies, whole, s1, r1)
             half = view(slice(None), slice(None), mk)
             landing = half if out_view is None else out_view(slice(None), slice(None), mk)
             self.third = remote(half, landing, s3, r3, k_peer)
@@ -230,7 +250,8 @@
                 self.local = pltpu.make_async_copy(half, landing, out_sem)
 
         def start1(self):
-            self.first.wait_recv()
+            if self.first is not None:
+                self.first.wait_recv()
             self.near.start()
 
         def start3(self):
@@ -240,7 +261,8 @@
                 self.local.start()
 
         def finish(self):
-            self.first.wait_send()
+            if self.first is not None:
+                self.first.wait_send()
             self.near.wait_send()
             self.third.wait_send()
             if self.local is not None:
@@ -257,6 +279,7 @@
         Direct(
             lambda z, h, k, half=half: ag_a.at[0, half, z, h, k],
             direct_sems(half),
+            plane=True,
         )
         for half in range(2)
     ]
@@ -268,20 +291,20 @@
         for c in range(1, CH)
     ]
     def pick_gather(n, first, count):
-        return Direct(
-            lambda z, h, k: ag_b.at[z, h, k, :, pl.ds(first, count)],
-            direct_sems(2 + n),
-            lambda z, h, k: pick_hbm.at[z, h, k, :, pl.ds(first, count)],
-            out_sem.at[2, n],
-        )
+        view = lambda z, h, k: ag_b.at[z, h, k, :, pl.ds(first, count)]
+        out_view = lambda z, h, k: pick_hbm.at[z, h, k, :, pl.ds(first, count)]
+        if n == CH - 2:
+            sems = pair_sems(CH - 1, a1s, a1r, a2s, a2r, a3s, a3r)
+            return Gather(view, sems, out_view, out_sem.at[2, n])
+        return Direct(view, direct_sems(2 + n), out_view, out_sem.at[2, n], plane=n == CH)
 
     db = [pick_gather(c, c * 1024, 1024) for c in range(CH - 1)]
     db = db + [pick_gather(CH - 1 + half, 3072 + half * 512, 512) for half in range(2)]
 
     pl.semaphore_wait(barrier, len(peers))
-    for gather in da + ga[1:]:
+    da[0].start1()
+    for gather in ga[1:]:
         gather.first.start()
-    da[0].start1()
 
     reach = LAG_FIRST + lax.broadcasted_iota(jnp.int32, (LAG_HALF, 128), 0)
     first, last = cs_ref[...], ce_ref[...]
@@ -308,24 +331,18 @@
         return [Group(copies, whole, ssem.at[n], rsem.at[n])]
 
     whole_half = send1.at[0, pl.ds(0, 4 * (NF - 1)), pl.ds(0, 16), :]
-    whole_full = send1.at[0, pl.ds(0, 4 * (NF - 1))]
 
     ex1 = [
-        exchange(
-            half,
-            lambda j, half=half: send1.at[0, quad(j), pl.ds(half * 16, 16), :],
-            lambda j, half=half: recv1.at[0, :, part_rows(j, half), :],
-            whole_half, x1s, x1r,
-        )
-        for half in range(2)
-    ] + [
-        exchange(
-            c + 1,
-            lambda j, c=c: send1.at[c, quad(j)],
-            lambda j, c=c: recv1.at[c, :, rows(j), :],
-            whole_full, x1s, x1r,
-        )
-        for c in range(1, CH)
+        [
+            exchange(
+                2 * c + half,
+                lambda j, c=c, half=half: send1.at[c, quad(j), pl.ds(half * 16, 16), :],
+                lambda j, c=c, half=half: recv1.at[c, :, part_rows(j, half), :],
+                whole_half, x1s, x1r,
+            )
+            for half in range(2)
+        ]
+        for c in range(CH)
     ]
     ex2 = [
         [
@@ -381,18 +398,18 @@
     def cross_first(half):
         da[half].third.wait_recv()
         cross_half(0, half)
-        send(ex1[half])
+        send(ex1[0][half])
         recv1[0, :, part_rows(mf, half), :] = send1[0, quad(mf), half * 16 : half * 16 + 16, :]
 
     def cross(c):
         ga[c].third.wait_recv()
-        cross_half(c, 0)
-        cross_half(c, 1)
-        send(ex1[c + 1])
+        for half in range(2):
+            cross_half(c, half)
+            send(ex1[c][half])
         recv1[c, :, rows(mf), :] = send1[c, quad(mf)]
 
     def lag_step(c):
-        for copy in ex1[0] + ex1[1] if c == 0 else ex1[c + 1]:
+        for copy in ex1[c][0] + ex1[c][1]:
             copy.wait_recv()
 
         def two_sources(pair, _):
@@ -448,7 +465,10 @@
         for copy in ex2[CH - 1][half]:
             copy.wait_recv()
         turn_half(CH - 1, half)
-        db[CH - 1 + half].first.start()
+        if half == 0:
+            db[CH - 1].first.start()
+        else:
+            db[CH].start1()
 
     da[0].start3()
     ga[1].start1()
@@ -475,12 +495,13 @@
     give_back(1, 0)
     for gather in da + ga[1:]:
         gather.finish()
-    sent(ex1[0] + ex1[1] + ex1[2] + ex1[3])
+    for c in range(CH - 1):
+        sent(ex1[c][0] + ex1[c][1])
     turn_step(0)
     give_back(1, 1)
     lag_step(2)
     give_back(2, 0)
-    sent(ex1[4] + ex2[0][0] + ex2[0][1])
+    sent(ex1[3][0] + ex1[3][1] + ex2[0][0] + ex2[0][1])
     db[0].start1()
     turn_step(1)
     give_back(2, 1)
@@ -497,7 +518,7 @@
     db[1].start3()
     turn_last(1)
     db[3].start1()
-    db[4].start1()
+    db[2].start2()
     sent(ex2[2][0] + ex2[2][1])
     db[1].finish()
     db[2].start3()
@@ -539,7 +560,7 @@
     smem = pl.BlockSpec(memory_space=pltpu.SMEM)
     hbm = pl.BlockSpec(memory_space=pl.ANY)
     dma = pltpu.SemaphoreType.DMA
-    gather_sems = [dma((CH - 1,))] * 3 + [dma((CH - 1, 3))] + [dma((CH - 1,))] * 2
+    gather_sems = [dma((CH,))] * 3 + [dma((CH, 3))] + [dma((CH,))] * 2
     rel, picked = pl.pallas_call(
         c3_kernel,
         out_shape=(
@@ -574,8 +595,7 @@
         + [dma((CH + 3,))] * 2
         + [dma((CH + 3,))] * 2
         + [dma((CH + 3,))] * 2
-        + [dma((CH + 1,))] * 2
-        + [dma((2 * CH,))] * 2,
+        + [dma((2 * CH,))] * 4,
         compiler_params=pltpu.CompilerParams(
             collective_id=0, has_side_effects=True, vmem_limit_bytes=56 << 20
         ),

time: 98.4 us -> 94.2 us (0.957)
  Pallas kernels: 98.3 us -> 94.1 us
    pallas_call x1, Pallas kernels: 92.6 us -> 88.4 us  [per_device(): pl.pallas_call(c3_kernel, out_shape=(jax.ShapeDtypeStruct((16, 256, 256),...]
where the time goes in v4:
time: 94.2 us; the launch traced here: 94.1 us
  Pallas kernels  94.1 us (100%)
    pallas_call x1, Pallas kernels, per_device(): pl.pallas_call(c3_kernel, out_shape=(jax.ShapeDtypeStruct((16, 256, 256),...  88.4 us
    pallas_call x1, Pallas kernels, per_device(): pl.pallas_call(functools.partial(final_kernel, 1.0 / math.sqrt(sources)),...  5.7 us

profile of v4, /device:TPU:1, one launch (start us, length us, event | category | flops | bytes accessed | tf_op | source)
XLA Modules:
  0.0 94.1 jit_solution(17732992418452130846)
XLA Ops:
  0.0 88.4 %c3_exchange.1 = (bf16[16,256,256]{2,1,0:T(8,128)(2,1)}, bf16[8,2,2,8,4096]{4,3,2,1,0:T(8,128)(2,1)}) custom-call(s32[128]{0:T(128)} %vs_ref.1, s32[256]{0:T(256)} %rf_ref.1, s32[1,128]{1,0:T(1,128)} %bitcast.9, s32[1,128]{1,0:T(1,128)} %bitcast.10, bf16[896,256]{1,0:T(8,128)(2,1)} %constant.8.clone.inv_hbm, bf16[256,896]{1,0:T(8,128)(2,1)} %constant.9.clone.fwd_hbm, ...), custom_call_target="tpu_custom_call" | custom-call | tf_op jit(solution)/shard_map/c3_exchange/pallas_call | solution.py:564
  88.5 5.7 %recorrelate.1 = f32[2,16,256,256]{3,2,1,0:T(8,128)} custom-call(bf16[256,4096]{1,0:T(8,128)(2,1)} %bitcast.4, bf16[256,4096]{1,0:T(8,128)(2,1)} %bitcast.5, bf16[256,4096]{1,0:T(8,128)(2,1)} %bitcast.6, bf16[256,4096]{1,0:T(8,128)(2,1)} %bitcast.7, bf16[16,256,256]{2,1,0:T(8,128)(2,1)} %get-tuple-element.8.rel_ref), custom_call_target="tpu_custom_call" | custom-call | tf_op jit(solution)/shard_map/recorrelate/pallas_call | solution.py:619

commit v5 on v4

--- a/solution.py
+++ b/solution.py
@@ -296,7 +296,7 @@
         if n == CH - 2:
             sems = pair_sems(CH - 1, a1s, a1r, a2s, a2r, a3s, a3r)
             return Gather(view, sems, out_view, out_sem.at[2, n])
-        return Direct(view, direct_sems(2 + n), out_view, out_sem.at[2, n], plane=n == CH)
+        return Direct(view, direct_sems(2 + n), out_view, out_sem.at[2, n], plane=n >= CH - 1)
 
     db = [pick_gather(c, c * 1024, 1024) for c in range(CH - 1)]
     db = db + [pick_gather(CH - 1 + half, 3072 + half * 512, 512) for half in range(2)]
@@ -465,10 +465,7 @@
         for copy in ex2[CH - 1][half]:
             copy.wait_recv()
         turn_half(CH - 1, half)
-        if half == 0:
-            db[CH - 1].first.start()
-        else:
-            db[CH].start1()
+        db[CH - 1 + half].start1()
 
     da[0].start3()
     ga[1].start1()
@@ -517,7 +514,6 @@
     turn_last(0)
     db[1].start3()
     turn_last(1)
-    db[3].start1()
     db[2].start2()
     sent(ex2[2][0] + ex2[2][1])
     db[1].finish()

time: 94.2 us -> 94.4 us (level)
  no operation moved by 1% of the time
where the time goes in v5:
time: 94.4 us; the launch traced here: 94.3 us
  Pallas kernels  94.3 us (100%)
    pallas_call x1, Pallas kernels, per_device(): pl.pallas_call(c3_kernel, out_shape=(jax.ShapeDtypeStruct((16, 256, 256),...  88.6 us
    pallas_call x1, Pallas kernels, per_device(): pl.pallas_call(functools.partial(final_kernel, 1.0 / math.sqrt(sources)),...  5.69 us

profile of v5, /device:TPU:1, one launch (start us, length us, event | category | flops | bytes accessed | tf_op | source)
XLA Modules:
  0.0 94.3 jit_solution(11734667987975813406)
XLA Ops:
  0.0 88.6 %c3_exchange.1 = (bf16[16,256,256]{2,1,0:T(8,128)(2,1)}, bf16[8,2,2,8,4096]{4,3,2,1,0:T(8,128)(2,1)}) custom-call(s32[128]{0:T(128)} %vs_ref.1, s32[256]{0:T(256)} %rf_ref.1, s32[1,128]{1,0:T(1,128)} %bitcast.9, s32[1,128]{1,0:T(1,128)} %bitcast.10, bf16[896,256]{1,0:T(8,128)(2,1)} %constant.8.clone.inv_hbm, bf16[256,896]{1,0:T(8,128)(2,1)} %constant.9.clone.fwd_hbm, ...), custom_call_target="tpu_custom_call" | custom-call | tf_op jit(solution)/shard_map/c3_exchange/pallas_call | solution.py:560
  88.6 5.7 %recorrelate.1 = f32[2,16,256,256]{3,2,1,0:T(8,128)} custom-call(bf16[256,4096]{1,0:T(8,128)(2,1)} %bitcast.4, bf16[256,4096]{1,0:T(8,128)(2,1)} %bitcast.5, bf16[256,4096]{1,0:T(8,128)(2,1)} %bitcast.6, bf16[256,4096]{1,0:T(8,128)(2,1)} %bitcast.7, bf16[16,256,256]{2,1,0:T(8,128)(2,1)} %get-tuple-element.8.rel_ref), custom_call_target="tpu_custom_call" | custom-call | tf_op jit(solution)/shard_map/recorrelate/pallas_call | solution.py:615
